TPU v7x, 32 devices: a whole 2x2x4 slice. The times are simulated.
32 devices in a mesh: node: 8 (over z, core), local: 4 (over y, x).
Axes of the slice: x: 2, y: 2, z: 4, core: 2. Of those that a mesh axis runs over, the one named last changes fastest.
Arguments:
- tokens: bfloat16 [64, 7168], P(('node', 'local')), may hold values from -6 to 6
- expert_ids: int32 [64, 8], P(('node', 'local')), may hold values from 0 to 31, all different within a row; in each aligned block of 8 rows (0 to 7, 8 to 15, ...) at most 4 rows name the same one
- gate_weights: bfloat16 [64, 8], P(('node', 'local')), may hold values from 0.049804688 to 1
- expert_seeds: int32 [32], P('node'), may hold values from 0 to 16777215
Outputs:
- moe_out: bfloat16 [64, 7168], P(('node', 'local'))
Inputs may be any that keep to these rules, and one draw needn't show every extreme that they name: `expert_ids`: each row names 8 different experts. Within the tokens of one node group (aligned blocks of 8 rows), no expert is named by more than 4 rows, a bound that some block reaches.
All inputs are finite; a program needn't handle non-finite values.
Results may differ from a plain program's by a relative error of at most 0.0078.
Values may be sent and summed in bfloat16 or wider, within the bound.
No kernel may reach another device: no remote copies, remote signals or barrier semaphores. Data moves between devices by JAX's collectives and lax.ppermute only.
A program may use at most 128 MiB of HBM per device.

v0:
```python
import math
import jax
import jax.numpy as jnp
from jax import lax
from jax.sharding import PartitionSpec as P

FF = 2048
TOP = 8
EXP_NODE = 4
mix_const = 73244475


def hashed_weights(expert_seed, matrix_code, row_ids, col_ids, col_count, fan_in):
    flat_index = row_ids[:, None] * col_count + col_ids[None, :]
    mixing = expert_seed + matrix_code * 1000003 + flat_index * 374761393
    mixing = mixing ^ jnp.right_shift(mixing, 16)
    mixing = mixing * mix_const
    mixing = mixing ^ jnp.right_shift(mixing, 15)
    mixing = mixing * mix_const
    mixing = mixing ^ jnp.right_shift(mixing, 16)
    uniform_part = (mixing & 16777215).astype(jnp.float32) * (1.0 / 16777216.0) - 0.5
    return (uniform_part * math.sqrt(12.0 / fan_in)).astype(jnp.bfloat16)


def block_weights(expert_seed, hidden_ids, model_width, hidden_total):
    feature_ids = jnp.arange(model_width, dtype=jnp.int32)
    gate_and_up = jnp.concatenate(
        [
            hashed_weights(expert_seed, 0, feature_ids, hidden_ids, hidden_total, model_width),
            hashed_weights(expert_seed, 1, feature_ids, hidden_ids, hidden_total, model_width),
        ],
        axis=1,
    )
    w_down = hashed_weights(expert_seed, 2, hidden_ids, feature_ids, model_width, hidden_total)
    return (gate_and_up, w_down)


def apply_block(row_block, gate_and_up, w_down):
    hidden_block = w_down.shape[0]
    projected = jnp.dot(row_block, gate_and_up, preferred_element_type=jnp.float32)
    hidden = (jax.nn.silu(projected[:, :hidden_block]) * projected[:, hidden_block:]).astype(
        jnp.bfloat16
    )
    return jnp.dot(hidden, w_down, preferred_element_type=jnp.float32)


def quarter_output(flat_rows, expert_seed, first_unit, quarter_width, hidden_block):
    model_width = flat_rows.shape[1]
    accumulated = jnp.zeros((flat_rows.shape[0], model_width), jnp.float32)
    for offset in range(0, quarter_width, hidden_block):
        hidden_ids = first_unit + offset + jnp.arange(hidden_block, dtype=jnp.int32)
        gate_and_up, w_down = block_weights(expert_seed, hidden_ids, model_width, FF)
        accumulated = accumulated + apply_block(flat_rows, gate_and_up, w_down)
    return accumulated.astype(jnp.bfloat16)


def body(tokens, expert_ids, gate_weights, expert_seeds):
    n_node = lax.axis_size("node")
    n_local = lax.axis_size("local")
    quarters = n_local // EXP_NODE
    quarter_width = FF // quarters
    hidden_block = min(quarter_width, 256)
    model_width = tokens.shape[1]
    group_rows, group_ids, group_gates = (
        lax.all_gather(tokens, "local", axis=0, tiled=True),
        lax.all_gather(expert_ids, "local", axis=0, tiled=True),
        lax.all_gather(gate_weights, "local", axis=0, tiled=True),
    )
    tok_node = group_rows.shape[0]
    capacity = 2 * tok_node * TOP // (EXP_NODE * n_node)
    local_index = lax.axis_index("local")
    expert_kind = local_index // quarters
    quarter = local_index % quarters
    targets = (
        jnp.arange(n_node, dtype=jnp.int32)[:, None] * EXP_NODE
        + jnp.arange(EXP_NODE, dtype=jnp.int32)[None, :]
    )
    id_match = group_ids[:, :, None, None] == targets[None, None, :, :]
    routed_hits = jnp.any(id_match, axis=1)
    picked = jnp.sum(
        jnp.where(id_match, group_gates.astype(jnp.float32)[:, :, None, None], 0.0), axis=1
    )
    counts = jnp.cumsum(routed_hits.astype(jnp.int32), axis=0) - 1
    slot_place = jnp.where(routed_hits, counts, -1)
    slot_select = (
        jnp.transpose(slot_place, (1, 2, 0))[:, :, None, :]
        == jnp.arange(capacity, dtype=jnp.int32)[None, None, :, None]
    )
    expert_seed = expert_seeds[expert_kind]
    first_unit = quarter * quarter_width
    own_select = lax.dynamic_index_in_dim(slot_select, expert_kind, 1, keepdims=False)
    own_picked = lax.dynamic_index_in_dim(picked, expert_kind, 2, keepdims=False)
    outgoing = jnp.einsum(
        "mct,td->mcd",
        own_select.astype(jnp.bfloat16),
        group_rows,
        preferred_element_type=jnp.float32,
    ).astype(jnp.bfloat16)
    arrived = lax.all_to_all(outgoing, "node", split_axis=0, concat_axis=0, tiled=True)
    row_total = arrived.shape[0] * arrived.shape[1]
    flat_rows = arrived.reshape(row_total, model_width)
    flat_out = quarter_output(flat_rows, expert_seed, first_unit, quarter_width, hidden_block)
    returned = lax.all_to_all(
        flat_out.reshape(arrived.shape), "node", split_axis=0, concat_axis=0, tiled=True
    )
    combine_weights = own_select.astype(jnp.float32) * own_picked.T[:, None, :]
    partial_term = jnp.einsum(
        "mct,mcd->td",
        combine_weights,
        returned.astype(jnp.float32),
        precision=lax.Precision.HIGHEST,
    )
    own_rows = lax.psum_scatter(partial_term, "local", scatter_dimension=0, tiled=True)
    return own_rows.astype(jnp.bfloat16)


def solution(mesh):
    return jax.shard_map(
        body,
        mesh=mesh,
        in_specs=(
            P(("node", "local"), None),
            P(("node", "local"), None),
            P(("node", "local"), None),
            P("node"),
        ),
        out_specs=P(("node", "local"), None),
        check_vma=False,
    )
```

profile of v0, /device:TPU:0, one launch (start us, length us, event | category | flops | bytes accessed | tf_op | source)
XLA Modules:
  0.0 199.2 jit_solution(6134852472920081447)
XLA Ops:
  0.0 10.1 %all-gather.2 = bf16[4,2,7168]{2,1,0:T(2,128)(2,1)S(1)} all-gather(bf16[1,2,7168]{2,1,0:T(2,128)(2,1)} %bitcast.32), channel_id=1, replica_groups=mesh['node'=8,'local'=4] {'local'}, dimensions={0}, use_global_device_ids=true | all-gather | bytes 143360 | tf_op jit(solution)/shard_map/all_gather | solution.py:65
  10.2 7.9 %all-gather = s32[4,2,8]{2,1,0:T(2,128)S(1)} all-gather(s32[1,2,8]{2,1,0:T(2,128)} %bitcast.35), channel_id=1, replica_groups=mesh['node'=8,'local'=4] {'local'}, dimensions={0}, use_global_device_ids=true | all-gather | bytes 320 | tf_op jit(solution)/shard_map/all_gather | solution.py:66
  18.1 0.1 compare_reduce_fusion
  18.2 0.1 copy.16
  18.3 0.3 convolution_convert_fusion
  18.6 1.1 copy.18
  19.7 4.9 %all-to-all-start = ((bf16[8,4,7168]{2,1,0:T(4,128)(2,1)}), bf16[8,4,7168]{2,1,0:T(4,128)(2,1)S(1)}, u32[]{:S(2)}, u32[]{:S(2)}) async-start(bf16[8,4,7168]{2,1,0:T(4,128)(2,1)} %copy.18), calls=%async_computation | async-start | bytes 917504 | tf_op jit(solution)/shard_map/all_to_all | solution.py:99
  24.6 1.2 dynamic_slice.13
  26.5 69.3 %fusion.176 = (bf16[7168,256]{1,0:T(8,128)(2,1)}, bf16[7168,256]{1,0:T(8,128)(2,1)}, bf16[7168,256]{1,0:T(8,128)(2,1)}, bf16[7168,256]{1,0:T(8,128)(2,1)}, bf16[...) fusion(s32[256]{0:T(256)S(1)} %get-tuple-element.33, ...), kind=kLoop, calls=%fused_computation.257 | loop fusion | flops 469762048 | bytes 58756104 | tf_op jit(solution)/shard_map/convert_element_type | solution.py:22
  96.6 0.1 reshape.115
  96.8 4.5 %fusion.193 = f32[32,512]{1,0:T(8,128)S(1)} fusion(bf16[32,7168]{1,0:T(8,128)(2,1)S(1)} %reshape.115, bf16[7168,256]{1,0:T(8,128)(2,1)} %get-tuple-element.31, bf16[7168,256]{1,0:T(8,128)(2,1)} %get-tuple-element.32), kind=kOutput, calls=%fused_computation.274 | convolution fusion | flops 249561088 | bytes 7864320 | tf_op jit(solution)/shard_map/dot_general | solution.py:40
  101.3 0.7 copy-done.13
  102.1 1.3 fusion.197
  103.4 0.7 copy-done.10
  104.1 1.1 copy-done.11
  105.2 1.3 fusion.201
  106.6 0.7 copy-done.8
  107.3 1.1 copy-done.9
  108.4 1.3 fusion.205
  109.7 0.7 copy-done.6
  110.4 1.1 copy-done.7
  111.5 1.3 fusion.209
  112.9 0.7 copy-done.4
  113.6 1.1 copy-done.5
  114.7 1.3 fusion.213
  116.0 0.7 copy-done.2
  116.7 1.1 copy-done.3
  117.9 1.3 fusion.217
  119.2 0.7 copy-done
  119.9 1.1 copy-done.1
  121.0 1.3 fusion.221
  122.4 4.4 %fusion.302 = f32[32,7168]{1,0:T(8,128)S(1)} fusion(s32[256]{0:T(256)S(1)} %iota_multiply_fusion.1, s32[]{:T(128)S(6)} %add.686, f32[32,512]{1,0:T(8,128)S(1)} %fusion.193), kind=kOutput, calls=%fused_computation.384 | convolution fusion | flops 148684800 | bytes 984068 | tf_op jit(solution)/shard_map/dot_general | solution.py:44
  126.8 4.6 %convolution_add_fusion.6 = f32[32,7168]{1,0:T(8,128)S(1)} fusion(f32[32,7168]{1,0:T(8,128)S(1)} %fusion.302, s32[256]{0:T(256)S(1)} %broadcast_multiply_fusion.6, s32[]{:T(128)S(6)} %add.686, f32[32,512]{1,0:T(8,128)S(1)} %fusion.197), kind=kOutput, calls=%fused_computation.78 | convolution fusion | flops 148914176 | bytes 1901572 | tf_op jit(solution)/shard_map/dot_general | solution.py:44
  131.4 4.4 %convolution_add_fusion.5 = f32[32,7168]{1,0:T(8,128)S(1)} fusion(f32[32,7168]{1,0:T(8,128)S(1)} %convolution_add_fusion.6, s32[256]{0:T(256)S(1)} %broadcast_multiply_fusion.5, s32[]{:T(128)S(6)} %add.686, f32[32,512]{1,0:T(8,128)S(1)} %fusion.201), kind=kOutput, calls=%fused_computation.77 | convolution fusion | flops 148914176 | bytes 1901572 | tf_op jit(solution)/shard_map/dot_general | solution.py:44
  135.8 4.4 %convolution_add_fusion.4 = f32[32,7168]{1,0:T(8,128)S(1)} fusion(f32[32,7168]{1,0:T(8,128)S(1)} %convolution_add_fusion.5, s32[256]{0:T(256)S(1)} %broadcast_multiply_fusion.4, s32[]{:T(128)S(6)} %add.686, f32[32,512]{1,0:T(8,128)S(1)} %fusion.205), kind=kOutput, calls=%fused_computation.76 | convolution fusion | flops 148914176 | bytes 1901572 | tf_op jit(solution)/shard_map/dot_general | solution.py:44
  140.3 4.7 %convolution_add_fusion.3 = f32[32,7168]{1,0:T(8,128)S(1)} fusion(f32[32,7168]{1,0:T(8,128)S(1)} %convolution_add_fusion.4, s32[256]{0:T(256)S(1)} %broadcast_multiply_fusion.3, s32[]{:T(128)S(6)} %add.686, f32[32,512]{1,0:T(8,128)S(1)} %fusion.209), kind=kOutput, calls=%fused_computation.75 | convolution fusion | flops 148914176 | bytes 1901572 | tf_op jit(solution)/shard_map/dot_general | solution.py:44
  144.9 4.4 %convolution_add_fusion.2 = f32[32,7168]{1,0:T(8,128)S(1)} fusion(f32[32,7168]{1,0:T(8,128)S(1)} %convolution_add_fusion.3, s32[256]{0:T(256)S(1)} %broadcast_multiply_fusion.2, s32[]{:T(128)S(6)} %add.686, f32[32,512]{1,0:T(8,128)S(1)} %fusion.213), kind=kOutput, calls=%fused_computation.74 | convolution fusion | flops 148914176 | bytes 1901572 | tf_op jit(solution)/shard_map/dot_general | solution.py:44
  149.4 4.7 %convolution_add_fusion.1 = f32[32,7168]{1,0:T(8,128)S(1)} fusion(f32[32,7168]{1,0:T(8,128)S(1)} %convolution_add_fusion.2, s32[256]{0:T(256)S(1)} %broadcast_multiply_fusion.1, s32[]{:T(128)S(6)} %add.686, f32[32,512]{1,0:T(8,128)S(1)} %fusion.217), kind=kOutput, calls=%fused_computation.73 | convolution fusion | flops 148914176 | bytes 1901572 | tf_op jit(solution)/shard_map/dot_general | solution.py:44
  154.1 4.5 %fusion = bf16[32,7168]{1,0:T(8,128)(2,1)S(1)} fusion(f32[32,7168]{1,0:T(8,128)S(1)} %convolution_add_fusion.1, s32[256]{0:T(256)S(1)} %broadcast_multiply_fusion, s32[]{:T(128)S(6)} %add.686, f32[32,512]{1,0:T(8,128)S(1)} %fusion.221), kind=kOutput, calls=%fused_computation.79 | convolution fusion | flops 149143552 | bytes 1442820 | tf_op jit(solution)/shard_map/dot_general | solution.py:44
  158.6 1.0 reshape.116
  159.5 5.1 %all-to-all-start.1 = ((bf16[8,4,7168]{2,1,0:T(4,128)(2,1)}), bf16[8,4,7168]{2,1,0:T(4,128)(2,1)S(1)}, u32[]{:S(2)}, u32[]{:S(2)}) async-start(bf16[8,4,7168]{2,1,0:T(4,128)(2,1)} %reshape.116), calls=%async_computation.1 | async-start | bytes 917504 | tf_op jit(solution)/shard_map/all_to_all | solution.py:103
  164.6 7.2 %all-gather.1 = bf16[4,2,8]{2,1,0:T(2,128)(2,1)S(1)} all-gather(bf16[1,2,8]{2,1,0:T(2,128)(2,1)S(1)} %bitcast.36), channel_id=1, replica_groups=mesh['node'=8,'local'=4] {'local'}, dimensions={0}, use_global_device_ids=true | all-gather | bytes 160 | tf_op jit(solution)/shard_map/all_gather | solution.py:67
  171.8 0.1 fusion.307
  172.0 0.6 dynamic-slice
  173.3 5.3 %all-to-all-done.1 = bf16[8,4,7168]{2,1,0:T(4,128)(2,1)S(1)} async-done(((bf16[8,4,7168]{2,1,0:T(4,128)(2,1)}), bf16[8,4,7168]{2,1,0:T(4,128)(2,1)S(1)}, u32[]{:S(2)}, u32[]{:S(2)}) %all-to-all-start.1) | async-done | bytes 458784 | tf_op jit(solution)/shard_map/all_to_all | solution.py:103
  178.6 0.4 convolution_bitcast_fusion
  178.9 19.3 %all-reduce.2 = bf16[8,7168]{1,0:T(8,128)(2,1)S(1)} all-reduce(f32[8,7168]{1,0:T(8,128)S(1)} %convolution_bitcast_fusion), channel_id=2, replica_groups=mesh['node'=8,'local'=4] {'local'}, use_global_device_ids=true, to_apply=%region_3.4.clone | all-reduce | flops 57344 | bytes 344064
  198.2 0.6 dynamic-slice_convert_fusion
  (41 shorter events, 0.2 us)
Async XLA Ops:
  19.7 76.9 %all-to-all-start = ((bf16[8,4,7168]{2,1,0:T(4,128)(2,1)}), bf16[8,4,7168]{2,1,0:T(4,128)(2,1)S(1)}, u32[]{:S(2)}, u32[]{:S(2)}) async-start(bf16[8,4,7168]{2,1,0:T(4,128)(2,1)} %copy.18), calls=%async_computation | async-start | bytes 917504 | tf_op jit(solution)/shard_map/all_to_all | solution.py:99
  96.7 4.6 %copy-start.12 = (bf16[7168,256]{1,0:T(8,128)(2,1)S(1)}, bf16[7168,256]{1,0:T(8,128)(2,1)}, u32[]{:S(2)}) copy-start(bf16[7168,256]{1,0:T(8,128)(2,1)} %get-tuple-element.19) | copy-start | bytes 11010052
  96.7 5.3 %copy-start.13 = (bf16[7168,256]{1,0:T(8,128)(2,1)S(1)}, bf16[7168,256]{1,0:T(8,128)(2,1)}, u32[]{:S(2)}) copy-start(bf16[7168,256]{1,0:T(8,128)(2,1)} %get-tuple-element.20) | copy-start | bytes 11010052
  102.1 2.0 %copy-start.10 = (bf16[7168,256]{1,0:T(8,128)(2,1)S(1)}, bf16[7168,256]{1,0:T(8,128)(2,1)}, u32[]{:S(2)}) copy-start(bf16[7168,256]{1,0:T(8,128)(2,1)} %get-tuple-element.21) | copy-start | bytes 11010052
  102.1 3.2 %copy-start.11 = (bf16[7168,256]{1,0:T(8,128)(2,1)S(1)}, bf16[7168,256]{1,0:T(8,128)(2,1)}, u32[]{:S(2)}) copy-start(bf16[7168,256]{1,0:T(8,128)(2,1)} %get-tuple-element.22) | copy-start | bytes 11010052
  105.2 2.0 %copy-start.8 = (bf16[7168,256]{1,0:T(8,128)(2,1)S(1)}, bf16[7168,256]{1,0:T(8,128)(2,1)}, u32[]{:S(2)}) copy-start(bf16[7168,256]{1,0:T(8,128)(2,1)} %get-tuple-element.23) | copy-start | bytes 11010052
  105.2 3.2 %copy-start.9 = (bf16[7168,256]{1,0:T(8,128)(2,1)S(1)}, bf16[7168,256]{1,0:T(8,128)(2,1)}, u32[]{:S(2)}) copy-start(bf16[7168,256]{1,0:T(8,128)(2,1)} %get-tuple-element.24) | copy-start | bytes 11010052
  108.4 2.0 %copy-start.6 = (bf16[7168,256]{1,0:T(8,128)(2,1)S(1)}, bf16[7168,256]{1,0:T(8,128)(2,1)}, u32[]{:S(2)}) copy-start(bf16[7168,256]{1,0:T(8,128)(2,1)} %get-tuple-element.25) | copy-start | bytes 11010052
  108.4 3.2 %copy-start.7 = (bf16[7168,256]{1,0:T(8,128)(2,1)S(1)}, bf16[7168,256]{1,0:T(8,128)(2,1)}, u32[]{:S(2)}) copy-start(bf16[7168,256]{1,0:T(8,128)(2,1)} %get-tuple-element.26) | copy-start | bytes 11010052
  111.5 2.0 %copy-start.4 = (bf16[7168,256]{1,0:T(8,128)(2,1)S(1)}, bf16[7168,256]{1,0:T(8,128)(2,1)}, u32[]{:S(2)}) copy-start(bf16[7168,256]{1,0:T(8,128)(2,1)} %get-tuple-element.27) | copy-start | bytes 11010052
  111.5 3.2 %copy-start.5 = (bf16[7168,256]{1,0:T(8,128)(2,1)S(1)}, bf16[7168,256]{1,0:T(8,128)(2,1)}, u32[]{:S(2)}) copy-start(bf16[7168,256]{1,0:T(8,128)(2,1)} %get-tuple-element.28) | copy-start | bytes 11010052
  114.7 2.0 %copy-start.2 = (bf16[7168,256]{1,0:T(8,128)(2,1)S(1)}, bf16[7168,256]{1,0:T(8,128)(2,1)}, u32[]{:S(2)}) copy-start(bf16[7168,256]{1,0:T(8,128)(2,1)} %get-tuple-element.29) | copy-start | bytes 11010052
  114.7 3.2 %copy-start.3 = (bf16[7168,256]{1,0:T(8,128)(2,1)S(1)}, bf16[7168,256]{1,0:T(8,128)(2,1)}, u32[]{:S(2)}) copy-start(bf16[7168,256]{1,0:T(8,128)(2,1)} %get-tuple-element.30) | copy-start | bytes 11010052
  117.8 2.0 %copy-start = (bf16[7168,256]{1,0:T(8,128)(2,1)S(1)}, bf16[7168,256]{1,0:T(8,128)(2,1)}, u32[]{:S(2)}) copy-start(bf16[7168,256]{1,0:T(8,128)(2,1)} %get-tuple-element.5) | copy-start | bytes 11010052
  117.8 3.2 %copy-start.1 = (bf16[7168,256]{1,0:T(8,128)(2,1)S(1)}, bf16[7168,256]{1,0:T(8,128)(2,1)}, u32[]{:S(2)}) copy-start(bf16[7168,256]{1,0:T(8,128)(2,1)} %get-tuple-element.6) | copy-start | bytes 11010052
  154.1 10.5 %copy-start.14 = (bf16[2,8]{1,0:T(2,128)(2,1)S(1)}, bf16[2,8]{1,0:T(2,128)(2,1)}, u32[]{:S(2)}) copy-start(bf16[2,8]{1,0:T(2,128)(2,1)} %param.6) | copy-start | bytes 100
  154.1 17.9 %copy-start.15 = (u32[32]{0:T(128)S(1)}, u32[32]{0:T(128)}, u32[]{:S(2)}) copy-start(u32[32]{0:T(128)} %constant.137) | copy-start | bytes 388
  159.5 19.0 %all-to-all-start.1 = ((bf16[8,4,7168]{2,1,0:T(4,128)(2,1)}), bf16[8,4,7168]{2,1,0:T(4,128)(2,1)S(1)}, u32[]{:S(2)}, u32[]{:S(2)}) async-start(bf16[8,4,7168]{2,1,0:T(4,128)(2,1)} %reshape.116), calls=%async_computation.1 | async-start | bytes 917504 | tf_op jit(solution)/shard_map/all_to_all | solution.py:103
where the time goes:
time: 203 us; the launch traced here: 199 us
  other arithmetic  69.7 us (34%)
  matrix products  50.8 us (25%)
  blocking collectives  44.5 us (22%)
  local copies, waits for them, and re-layouts  16.5 us (8%)
  starting transfers between devices  9.97 us (5%)
  waiting for transfers between devices  5.29 us (3%)
  between operations  2.45 us (1%)
    convert_element_type x1, other arithmetic, hashed_weights(): return (uniform_part * math.sqrt(12.0 / fan_in)).astype(jnp.bfloat16)  69.3 us
    dot_general x8, matrix products, apply_block(): return jnp.dot(hidden, w_down, preferred_element_type=jnp.float32)  36.2 us
    unnamed x1, blocking collectives  19.3 us
    dot_general x8, matrix products, apply_block(): jnp.dot(row_block, gate_and_up, preferred_element_type=jnp.float32)  14 us
    unnamed x34, local copies, waits for them, and re-layouts  12.2 us
    all_gather x1, blocking collectives, body(): lax.all_gather(tokens, 'local', axis=0, tiled=True)  10.1 us
    all_gather x1, blocking collectives, body(): lax.all_gather(expert_ids, 'local', axis=0, tiled=True)  7.86 us
    all_gather x1, blocking collectives, body(): lax.all_gather(gate_weights, 'local', axis=0, tiled=True)  7.17 us
  transfers between devices with their start and end apart: 2, of which 1 were waited for; matrix products, arithmetic and copies ran while one was open for 36% of the time, Pallas kernels for 0%

commit v1 on v0

--- a/solution.py
+++ b/solution.py
@@ -62,7 +62,12 @@
     hidden_block = min(quarter_width, 256)
     model_width = tokens.shape[1]
     group_rows, group_ids, group_gates = (
-        lax.all_gather(tokens, "local", axis=0, tiled=True),
+        jnp.concatenate(
+            lax.all_to_all(
+                jnp.stack([tokens for _ in range(lax.axis_size("local"))], axis=0), "local", 0, 0
+            ),
+            axis=0,
+        ),
         lax.all_gather(expert_ids, "local", axis=0, tiled=True),
         lax.all_gather(gate_weights, "local", axis=0, tiled=True),
     )

time: 203 us -> 212 us (1.044)
  waiting for transfers between devices: 5.29 us -> 17.8 us
  blocking collectives: 44.5 us -> 36 us
  starting transfers between devices: 9.97 us -> 13.5 us
    all_to_all x1, waiting for transfers between devices: 0.01 us -> 13.2 us  [body(): lax.all_to_all(outgoing, 'node', split_axis=0, concat_axis=0, tiled=True)]
    all_gather x1 -> x0, blocking collectives: 10.1 us -> none  [body(): lax.all_gather(tokens, 'local', axis=0, tiled=True)]
    all_to_all x0 -> x1, starting transfers between devices: none -> 5.19 us  [body(): lax.all_to_all(jnp.stack([tokens for _ in range(lax.axis_size('local'))],...]
    unnamed x34 -> x33, local copies, waits for them, and re-layouts: 12.2 us -> 12.2 us
  transfers between devices with their start and end apart: 2 -> 3, of which waited for: 1 -> 2; matrix products, arithmetic and copies ran while one was open for 36% -> 34% of each run, Pallas kernels for 0% -> 0%
where the time goes in v1:
time: 212 us; the launch traced here: 208 us
  other arithmetic  69.6 us (33%)
  matrix products  50.8 us (24%)
  blocking collectives  36 us (17%)
  local copies, waits for them, and re-layouts  17.9 us (8%)
  waiting for transfers between devices  17.8 us (8%)
  starting transfers between devices  13.5 us (6%)
  between operations  2.46 us (1%)
    convert_element_type x1, other arithmetic, hashed_weights(): return (uniform_part * math.sqrt(12.0 / fan_in)).astype(jnp.bfloat16)  69.3 us
    dot_general x8, matrix products, apply_block(): return jnp.dot(hidden, w_down, preferred_element_type=jnp.float32)  36.2 us
    unnamed x1, blocking collectives  19.5 us
    dot_general x8, matrix products, apply_block(): jnp.dot(row_block, gate_and_up, preferred_element_type=jnp.float32)  14 us
    all_to_all x1, waiting for transfers between devices, body(): lax.all_to_all(outgoing, 'node', split_axis=0, concat_axis=0, tiled=True)  13.2 us
    unnamed x33, local copies, waits for them, and re-layouts  12.2 us
    all_gather x1, blocking collectives, body(): lax.all_gather(expert_ids, 'local', axis=0, tiled=True)  8.7 us
    all_gather x1, blocking collectives, body(): lax.all_gather(gate_weights, 'local', axis=0, tiled=True)  7.79 us
  transfers between devices with their start and end apart: 3, of which 2 were waited for; matrix products, arithmetic and copies ran while one was open for 34% of the time, Pallas kernels for 0%

profile of v1, /device:TPU:0, one launch (start us, length us, event | category | flops | bytes accessed | tf_op | source)
XLA Modules:
  0.0 208.1 jit_solution(17723465393329281470)
XLA Ops:
  0.0 1.4 stack.2
  1.4 5.2 %all-to-all-start = ((bf16[4,2,7168]{2,1,0:T(2,128)(2,1)}), bf16[4,2,7168]{2,1,0:T(2,128)(2,1)S(1)}, u32[]{:S(2)}, u32[]{:S(2)}) async-start(bf16[4,2,7168]{2,1,0:T(2,128)(2,1)} %stack.2), calls=%async_computation | async-start | bytes 229376 | tf_op jit(solution)/shard_map/all_to_all | solution.py:66
  6.7 8.7 %all-gather = s32[4,2,8]{2,1,0:T(2,128)S(1)} all-gather(s32[1,2,8]{2,1,0:T(2,128)} %bitcast.33), channel_id=1, replica_groups=mesh['node'=8,'local'=4] {'local'}, dimensions={0}, use_global_device_ids=true | all-gather | bytes 320 | tf_op jit(solution)/shard_map/all_gather | solution.py:71
  15.4 0.1 compare_reduce_fusion
  15.6 1.2 dynamic_slice.13
  17.5 69.3 %fusion.176 = (bf16[7168,256]{1,0:T(8,128)(2,1)}, bf16[7168,256]{1,0:T(8,128)(2,1)}, bf16[7168,256]{1,0:T(8,128)(2,1)}, bf16[7168,256]{1,0:T(8,128)(2,1)}, bf16[...) fusion(s32[256]{0:T(256)S(1)} %get-tuple-element.33, ...), kind=kLoop, calls=%fused_computation.257 | loop fusion | flops 469762048 | bytes 58756104 | tf_op jit(solution)/shard_map/convert_element_type | solution.py:22
  86.9 0.2 convolution_convert_fusion
  87.2 1.1 copy.18
  88.3 4.9 %all-to-all-start.1 = ((bf16[8,4,7168]{2,1,0:T(4,128)(2,1)}), bf16[8,4,7168]{2,1,0:T(4,128)(2,1)S(1)}, u32[]{:S(2)}, u32[]{:S(2)}) async-start(bf16[8,4,7168]{2,1,0:T(4,128)(2,1)} %copy.18), calls=%async_computation.1 | async-start | bytes 917504 | tf_op jit(solution)/shard_map/all_to_all | solution.py:104
  93.9 13.2 %all-to-all-done.1 = bf16[8,4,7168]{2,1,0:T(4,128)(2,1)S(1)} async-done(((bf16[8,4,7168]{2,1,0:T(4,128)(2,1)}), bf16[8,4,7168]{2,1,0:T(4,128)(2,1)S(1)}, u32[]{:S(2)}, u32[]{:S(2)}) %all-to-all-start.1) | async-done | bytes 458784 | tf_op jit(solution)/shard_map/all_to_all | solution.py:104
  107.2 4.5 %fusion.193 = f32[32,512]{1,0:T(8,128)S(1)} fusion(bf16[32,7168]{1,0:T(8,128)(2,1)S(1)} %reshape.121, bf16[7168,256]{1,0:T(8,128)(2,1)} %get-tuple-element.31, bf16[7168,256]{1,0:T(8,128)(2,1)} %get-tuple-element.32), kind=kOutput, calls=%fused_computation.274 | convolution fusion | flops 249561088 | bytes 7864320 | tf_op jit(solution)/shard_map/dot_general | solution.py:40
  111.8 0.7 copy-done.13
  112.5 1.3 fusion.197
  113.9 0.7 copy-done.10
  114.6 1.1 copy-done.11
  115.7 1.3 fusion.201
  117.0 0.7 copy-done.8
  117.7 1.1 copy-done.9
  118.8 1.3 fusion.205
  120.2 0.7 copy-done.6
  120.9 1.1 copy-done.7
  122.0 1.3 fusion.209
  123.3 0.7 copy-done.4
  124.0 1.1 copy-done.5
  125.2 1.3 fusion.213
  126.5 0.7 copy-done.2
  127.2 1.1 copy-done.3
  128.3 1.3 fusion.217
  129.7 0.7 copy-done
  130.4 1.1 copy-done.1
  131.5 1.3 fusion.221
  132.8 4.4 %fusion.302 = f32[32,7168]{1,0:T(8,128)S(1)} fusion(s32[256]{0:T(256)S(1)} %iota_multiply_fusion.1, s32[]{:T(128)S(6)} %add.686, f32[32,512]{1,0:T(8,128)S(1)} %fusion.193), kind=kOutput, calls=%fused_computation.384 | convolution fusion | flops 148684800 | bytes 984068 | tf_op jit(solution)/shard_map/dot_general | solution.py:44
  137.2 4.6 %convolution_add_fusion.6 = f32[32,7168]{1,0:T(8,128)S(1)} fusion(f32[32,7168]{1,0:T(8,128)S(1)} %fusion.302, s32[256]{0:T(256)S(1)} %broadcast_multiply_fusion.6, s32[]{:T(128)S(6)} %add.686, f32[32,512]{1,0:T(8,128)S(1)} %fusion.197), kind=kOutput, calls=%fused_computation.78 | convolution fusion | flops 148914176 | bytes 1901572 | tf_op jit(solution)/shard_map/dot_general | solution.py:44
  141.9 4.4 %convolution_add_fusion.5 = f32[32,7168]{1,0:T(8,128)S(1)} fusion(f32[32,7168]{1,0:T(8,128)S(1)} %convolution_add_fusion.6, s32[256]{0:T(256)S(1)} %broadcast_multiply_fusion.5, s32[]{:T(128)S(6)} %add.686, f32[32,512]{1,0:T(8,128)S(1)} %fusion.201), kind=kOutput, calls=%fused_computation.77 | convolution fusion | flops 148914176 | bytes 1901572 | tf_op jit(solution)/shard_map/dot_general | solution.py:44
  146.3 4.4 %convolution_add_fusion.4 = f32[32,7168]{1,0:T(8,128)S(1)} fusion(f32[32,7168]{1,0:T(8,128)S(1)} %convolution_add_fusion.5, s32[256]{0:T(256)S(1)} %broadcast_multiply_fusion.4, s32[]{:T(128)S(6)} %add.686, f32[32,512]{1,0:T(8,128)S(1)} %fusion.205), kind=kOutput, calls=%fused_computation.76 | convolution fusion | flops 148914176 | bytes 1901572 | tf_op jit(solution)/shard_map/dot_general | solution.py:44
  150.8 4.7 %convolution_add_fusion.3 = f32[32,7168]{1,0:T(8,128)S(1)} fusion(f32[32,7168]{1,0:T(8,128)S(1)} %convolution_add_fusion.4, s32[256]{0:T(256)S(1)} %broadcast_multiply_fusion.3, s32[]{:T(128)S(6)} %add.686, f32[32,512]{1,0:T(8,128)S(1)} %fusion.209), kind=kOutput, calls=%fused_computation.75 | convolution fusion | flops 148914176 | bytes 1901572 | tf_op jit(solution)/shard_map/dot_general | solution.py:44
  155.4 4.4 %convolution_add_fusion.2 = f32[32,7168]{1,0:T(8,128)S(1)} fusion(f32[32,7168]{1,0:T(8,128)S(1)} %convolution_add_fusion.3, s32[256]{0:T(256)S(1)} %broadcast_multiply_fusion.2, s32[]{:T(128)S(6)} %add.686, f32[32,512]{1,0:T(8,128)S(1)} %fusion.213), kind=kOutput, calls=%fused_computation.74 | convolution fusion | flops 148914176 | bytes 1901572 | tf_op jit(solution)/shard_map/dot_general | solution.py:44
  159.9 4.7 %convolution_add_fusion.1 = f32[32,7168]{1,0:T(8,128)S(1)} fusion(f32[32,7168]{1,0:T(8,128)S(1)} %convolution_add_fusion.2, s32[256]{0:T(256)S(1)} %broadcast_multiply_fusion.1, s32[]{:T(128)S(6)} %add.686, f32[32,512]{1,0:T(8,128)S(1)} %fusion.217), kind=kOutput, calls=%fused_computation.73 | convolution fusion | flops 148914176 | bytes 1901572 | tf_op jit(solution)/shard_map/dot_general | solution.py:44
  164.6 4.5 %fusion = bf16[32,7168]{1,0:T(8,128)(2,1)S(1)} fusion(f32[32,7168]{1,0:T(8,128)S(1)} %convolution_add_fusion.1, s32[256]{0:T(256)S(1)} %broadcast_multiply_fusion, s32[]{:T(128)S(6)} %add.686, f32[32,512]{1,0:T(8,128)S(1)} %fusion.221), kind=kOutput, calls=%fused_computation.79 | convolution fusion | flops 149143552 | bytes 1442820 | tf_op jit(solution)/shard_map/dot_general | solution.py:44
  169.0 0.9 reshape.122
  170.0 3.5 %all-to-all-start.2 = ((bf16[8,4,7168]{2,1,0:T(4,128)(2,1)}), bf16[8,4,7168]{2,1,0:T(4,128)(2,1)S(1)}, u32[]{:S(2)}, u32[]{:S(2)}) async-start(bf16[8,4,7168]{2,1,0:T(4,128)(2,1)} %reshape.122), calls=%async_computation.2 | async-start | bytes 917504 | tf_op jit(solution)/shard_map/all_to_all | solution.py:108
  173.5 7.8 %all-gather.1 = bf16[4,2,8]{2,1,0:T(2,128)(2,1)S(1)} all-gather(bf16[1,2,8]{2,1,0:T(2,128)(2,1)S(1)} %bitcast.34), channel_id=1, replica_groups=mesh['node'=8,'local'=4] {'local'}, dimensions={0}, use_global_device_ids=true | all-gather | bytes 160 | tf_op jit(solution)/shard_map/all_gather | solution.py:72
  181.3 0.1 fusion.307
  181.5 0.6 dynamic-slice
  182.7 4.6 %all-to-all-done.2 = bf16[8,4,7168]{2,1,0:T(4,128)(2,1)S(1)} async-done(((bf16[8,4,7168]{2,1,0:T(4,128)(2,1)}), bf16[8,4,7168]{2,1,0:T(4,128)(2,1)S(1)}, u32[]{:S(2)}, u32[]{:S(2)}) %all-to-all-start.2) | async-done | bytes 458784 | tf_op jit(solution)/shard_map/all_to_all | solution.py:108
  187.3 0.4 convolution_bitcast_fusion
  187.7 19.5 %all-reduce.2 = bf16[8,7168]{1,0:T(8,128)(2,1)S(1)} all-reduce(f32[8,7168]{1,0:T(8,128)S(1)} %convolution_bitcast_fusion), channel_id=2, replica_groups=mesh['node'=8,'local'=4] {'local'}, use_global_device_ids=true, to_apply=%region_3.4.clone | all-reduce | flops 57344 | bytes 344064
  207.2 0.6 dynamic-slice_convert_fusion
  (43 shorter events, 0.4 us)
Async XLA Ops:
  1.4 85.4 %all-to-all-start = ((bf16[4,2,7168]{2,1,0:T(2,128)(2,1)}), bf16[4,2,7168]{2,1,0:T(2,128)(2,1)S(1)}, u32[]{:S(2)}, u32[]{:S(2)}) async-start(bf16[4,2,7168]{2,1,0:T(2,128)(2,1)} %stack.2), calls=%async_computation | async-start | bytes 229376 | tf_op jit(solution)/shard_map/all_to_all | solution.py:66
  88.3 18.8 %all-to-all-start.1 = ((bf16[8,4,7168]{2,1,0:T(4,128)(2,1)}), bf16[8,4,7168]{2,1,0:T(4,128)(2,1)S(1)}, u32[]{:S(2)}, u32[]{:S(2)}) async-start(bf16[8,4,7168]{2,1,0:T(4,128)(2,1)} %copy.18), calls=%async_computation.1 | async-start | bytes 917504 | tf_op jit(solution)/shard_map/all_to_all | solution.py:104
  107.2 4.6 %copy-start.12 = (bf16[7168,256]{1,0:T(8,128)(2,1)S(1)}, bf16[7168,256]{1,0:T(8,128)(2,1)}, u32[]{:S(2)}) copy-start(bf16[7168,256]{1,0:T(8,128)(2,1)} %get-tuple-element.19) | copy-start | bytes 11010052
  107.2 5.3 %copy-start.13 = (bf16[7168,256]{1,0:T(8,128)(2,1)S(1)}, bf16[7168,256]{1,0:T(8,128)(2,1)}, u32[]{:S(2)}) copy-start(bf16[7168,256]{1,0:T(8,128)(2,1)} %get-tuple-element.20) | copy-start | bytes 11010052
  112.5 2.0 copy-start.10
  112.5 3.2 %copy-start.11 = (bf16[7168,256]{1,0:T(8,128)(2,1)S(1)}, bf16[7168,256]{1,0:T(8,128)(2,1)}, u32[]{:S(2)}) copy-start(bf16[7168,256]{1,0:T(8,128)(2,1)} %get-tuple-element.22) | copy-start | bytes 11010052
  115.7 2.0 copy-start.8
  115.7 3.2 %copy-start.9 = (bf16[7168,256]{1,0:T(8,128)(2,1)S(1)}, bf16[7168,256]{1,0:T(8,128)(2,1)}, u32[]{:S(2)}) copy-start(bf16[7168,256]{1,0:T(8,128)(2,1)} %get-tuple-element.24) | copy-start | bytes 11010052
  118.8 2.0 copy-start.6
  118.8 3.2 %copy-start.7 = (bf16[7168,256]{1,0:T(8,128)(2,1)S(1)}, bf16[7168,256]{1,0:T(8,128)(2,1)}, u32[]{:S(2)}) copy-start(bf16[7168,256]{1,0:T(8,128)(2,1)} %get-tuple-element.26) | copy-start | bytes 11010052
  122.0 2.0 copy-start.4
  122.0 3.2 %copy-start.5 = (bf16[7168,256]{1,0:T(8,128)(2,1)S(1)}, bf16[7168,256]{1,0:T(8,128)(2,1)}, u32[]{:S(2)}) copy-start(bf16[7168,256]{1,0:T(8,128)(2,1)} %get-tuple-element.28) | copy-start | bytes 11010052
  125.2 2.0 copy-start.2
  125.2 3.2 %copy-start.3 = (bf16[7168,256]{1,0:T(8,128)(2,1)S(1)}, bf16[7168,256]{1,0:T(8,128)(2,1)}, u32[]{:S(2)}) copy-start(bf16[7168,256]{1,0:T(8,128)(2,1)} %get-tuple-element.30) | copy-start | bytes 11010052
  128.3 2.0 copy-start
  128.3 3.2 %copy-start.1 = (bf16[7168,256]{1,0:T(8,128)(2,1)S(1)}, bf16[7168,256]{1,0:T(8,128)(2,1)}, u32[]{:S(2)}) copy-start(bf16[7168,256]{1,0:T(8,128)(2,1)} %get-tuple-element.6) | copy-start | bytes 11010052
  164.6 8.9 %copy-start.14 = (bf16[2,8]{1,0:T(2,128)(2,1)S(1)}, bf16[2,8]{1,0:T(2,128)(2,1)}, u32[]{:S(2)}) copy-start(bf16[2,8]{1,0:T(2,128)(2,1)} %param.6) | copy-start | bytes 100
  164.6 16.9 %copy-start.15 = (u32[32]{0:T(128)S(1)}, u32[32]{0:T(128)}, u32[]{:S(2)}) copy-start(u32[32]{0:T(128)} %constant.137) | copy-start | bytes 388
  170.0 17.3 %all-to-all-start.2 = ((bf16[8,4,7168]{2,1,0:T(4,128)(2,1)}), bf16[8,4,7168]{2,1,0:T(4,128)(2,1)S(1)}, u32[]{:S(2)}, u32[]{:S(2)}) async-start(bf16[8,4,7168]{2,1,0:T(4,128)(2,1)} %reshape.122), calls=%async_computation.2 | async-start | bytes 917504 | tf_op jit(solution)/shard_map/all_to_all | solution.py:108
